TPU v7x, 256 devices: a whole 4x4x8 slice. The times are simulated.
256 devices in a mesh: clus: 4 (over z_lo, core), sub: 64 (over x, z_hi, y).
Axes of the slice: x: 4, y: 4, z: 8 (z_hi: 4, z_lo: 2; z = z_hi * 2 + z_lo), core: 2. Of those that a mesh axis runs over, the one named last changes fastest.
Arguments:
- load: float32 [4, 64, 6, 256, 128], P('clus', 'sub'), may hold values from -30 to 30
- dual_op: float32 [4, 64, 1536, 1536], P('clus', 'sub'), may hold values from -6 to 17, as said below
- modes: float32 [4, 64, 32, 1536], P('clus', 'sub'), may hold values from -1 to 1
- face_map: int32 [4, 64, 3, 256], P('clus', 'sub'), may hold values from 0 to 255, each once within a row
- cluster: int32 [4, 64], P('clus', 'sub'), may hold values from 0 to 1, as said below
Outputs:
- multipliers: float32 [4, 64, 6, 256, 128], P('clus', 'sub')
- residual: float32 [4, 64, 6, 256, 128], P('clus', 'sub')
Inputs may be any that keep to these rules, and one draw needn't show every extreme that they name: `dual_op`: each subdomain's block is symmetric positive definite. `face_map`: each row of 256 entries names every row of the neighbour's face once. In every cluster group exactly half of the 64 subdomains belong to each of its two clusters.
All inputs are finite; a program needn't handle non-finite values.
Results may differ from a plain program's by a relative error of at most 0.00011.
Values sent between devices are 32-bit elements; how exact they have to be, the bound alone decides.
No kernel may reach another device: no remote copies, remote signals or barrier semaphores. Data moves between devices by JAX's collectives and lax.ppermute only.
A program may use at most 128 MiB of HBM per device.

v0:
```python
import jax
import jax.numpy as jnp
from jax import lax
from jax.sharding import PartitionSpec as P

FACE = 256
COLS = 128
ITERS = 3
ORDER = 1536
damping_factor = 0.8
highest = lax.Precision.HIGHEST


def with_halo(cells, sides, width):
    for axis, dim in sides:
        count = lax.axis_size(axis)
        head = lax.slice_in_dim(cells, 0, width, axis=dim)
        tail = lax.slice_in_dim(cells, cells.shape[dim] - width, cells.shape[dim], axis=dim)
        cells = jnp.concatenate(
            [
                lax.ppermute(tail, axis, [(i, (i + 1) % count) for i in range(count)]),
                cells,
                lax.ppermute(head, axis, [((i + 1) % count, i) for i in range(count)]),
            ],
            axis=dim,
        )
    return cells


def from_partner(array, axis, distance):
    return lax.ppermute(array, axis, [(i, i ^ 1 << distance) for i in range(lax.axis_size(axis))])


def partner_values(values, pairing, inverse):
    result = []
    for direction in range(3):
        plus_face = values[2 * direction]
        minus_face = values[2 * direction + 1]
        upward = jnp.take(plus_face, inverse[direction], axis=0)
        width = upward.shape[0]
        if direction == 0:
            arrived = with_halo(jnp.concatenate([minus_face, upward], axis=0), (("sub", 0),), width)
            from_minus = arrived[:width]
            from_plus = arrived[3 * width :]
        elif direction == 1:
            arrived = with_halo(
                jnp.concatenate([minus_face, upward], axis=0), (("clus", 0),), width
            )
            from_minus = arrived[:width]
            from_plus = arrived[3 * width :]
        else:
            bit_index = lax.axis_size("sub").bit_length() - 2
            arrived = from_partner(jnp.stack([upward, minus_face]), "sub", bit_index)
            from_minus = arrived[0]
            from_plus = arrived[1]
        plus_side = jnp.take(from_plus, pairing[direction], axis=0)
        result += [plus_side, from_minus]
    return jnp.stack(result)


def solve_one(lower_part, column_block):
    return jax.scipy.linalg.cho_solve((lower_part, True), column_block)


def per_device(load, dual_op, modes, face_map, cluster):
    values = load[0, 0]
    operator = dual_op[0, 0]
    mode_rows = modes[0, 0]
    pairing = face_map[0, 0]
    member = cluster[0, 0]
    inverse = jnp.argsort(pairing, axis=-1)
    plus_owned = pairing % 2 == 0
    minus_owned = jnp.broadcast_to(jnp.arange(FACE) % 2 == 1, plus_owned.shape)
    owned = jnp.stack([plus_owned, minus_owned], axis=1).reshape(6, FACE, 1).astype(jnp.float32)
    selector = (jnp.arange(2) == member).astype(jnp.float32)
    weighted = mode_rows * owned.reshape(1, ORDER)
    gram_terms = jnp.einsum("mn,kn->mk", weighted, mode_rows, precision=highest)
    gram_total = lax.psum(selector[:, None, None] * gram_terms[None], "sub")
    factor = jnp.linalg.cholesky(gram_total)
    residual = values * owned
    multipliers = jnp.zeros_like(values)
    for iteration in range(ITERS):
        projected = jnp.einsum(
            "mn,nc->mc", mode_rows, residual.reshape(ORDER, COLS), precision=highest
        )
        gathered = lax.psum(selector[:, None, None] * projected[None], "sub")
        coefficients = jax.vmap(solve_one)(factor, gathered)
        own_coeff = lax.dynamic_index_in_dim(coefficients, member, 0, keepdims=False)
        correction = jnp.einsum("mn,mc->nc", mode_rows, own_coeff, precision=highest).reshape(
            6, FACE, COLS
        )
        search = residual - owned * correction
        local_copy = search - (1.0 - owned) * partner_values(search, pairing, inverse)
        applied = jnp.dot(operator, local_copy.reshape(ORDER, COLS), precision=highest).reshape(
            6, FACE, COLS
        )
        assembled = owned * (applied - partner_values(applied, pairing, inverse))
        numerator, denominator = lax.psum(
            (jnp.sum(residual * search, axis=(0, 1)), jnp.sum(search * assembled, axis=(0, 1))),
            ("clus", "sub"),
        )
        step_size = damping_factor * numerator / denominator
        multipliers = multipliers + step_size * search
        residual = residual - step_size * assembled
    return (multipliers[None, None], residual[None, None])


def solution(mesh):
    placed = (
        P("clus", "sub", None, None, None),
        P("clus", "sub", None, None),
        P("clus", "sub", None, None),
        P("clus", "sub", None, None),
        P("clus", "sub"),
    )
    return jax.shard_map(
        per_device,
        mesh=mesh,
        in_specs=placed,
        out_specs=(P("clus", "sub", None, None, None), P("clus", "sub", None, None, None)),
        check_vma=False,
    )
```

profile of v0, /device:TPU:1, one launch (start us, length us, event | category | flops | bytes accessed | tf_op | source)
XLA Modules:
  0.0 1692.0 jit_solution(10219532640262902524)
XLA Ops:
  22.2 326.7 %all-reduce.3 = (f32[2,32,128]{2,1,0:T(8,128)S(1)}, f32[2,32,32]{1,2,0:T(8,128)S(1)}) all-reduce(f32[2,32,128]{2,1,0:T(8,128)S(1)} %broadcast_multiply_fusion.3, f32[2,32,32]{1,2,0:T(8,128)S(1)} %broadcast_multiply_fusion.4), channel_id=1, replica_groups=mesh['clus'=4,'sub'=64] {'sub'}, use_global_device_ids=true, to_apply=%region_3.4 | all-reduce | flops 10240 | bytes 81920 | tf_op jit(solution)/shard_map/psum | solution.py:86
  349.0 5.9 custom-call.9
  355.1 4.9 custom-call.12
  360.4 1.8 convolution_bitcast_fusion.2
  363.6 2.1 multiply_subtract_fusion.9
  366.9 1.9 slice_bitcast_fusion.19
  373.3 56.8 %collective-permute-start.3 = (f32[256,128]{0,1:T(8,128)}, f32[256,128]{0,1:T(8,128)}, u32[]{:S(2)}, u32[]{:S(2)}) collective-permute-start(f32[256,128]{0,1:T(8,128)} %broadcast_select_fusion.10), channel_id=1, source_target_pairs={{0,64},{64,128},{128,192},{192,0},{1,65},{65,129},{129,193},{193,1... | collective-permute-start | bytes 393224 | tf_op jit(solution)/shard_map/ppermute | solution.py:21
  430.1 8.1 collective-permute-start
  439.5 3.8 collective-permute-done
  445.8 1.6 bitcast_dynamic-update-slice_fusion.46
  448.0 1.6 bitcast_dynamic-update-slice_fusion.44
  454.5 12.2 fusion.6
  472.0 8.7 collective-permute-start.5
  487.9 7.4 collective-permute-done.6
  497.9 1.6 multiply_reduce_fusion.5
  500.7 77.2 %all-reduce.2 = (f32[128]{0:T(128)S(1)}, f32[128]{0:T(128)S(1)}) all-reduce(f32[128]{0:T(128)S(1)} %get-tuple-element.13, f32[128]{0:T(128)S(1)} %get-tuple-element.12), channel_id=1, replica_groups=mesh['clus'=4,'sub'=64] {'clus','sub'}, use_global_device_ids=true, to_apply=%region_8.11 | all-reduce | flops 256 | bytes 2048 | tf_op jit(solution)/shard_map/psum | solution.py:98
  581.6 316.0 %psum.74 = f32[2,32,128]{2,1,0:T(8,128)S(1)} all-reduce(f32[2,32,128]{2,1,0:T(8,128)S(1)} %broadcast_multiply_fusion.2), channel_id=1, replica_groups=mesh['clus'=4,'sub'=64] {'sub'}, use_global_device_ids=true, to_apply=%region_9.12 | all-reduce | flops 8192 | bytes 65536 | tf_op jit(solution)/shard_map/psum | solution.py:86
  900.0 2.3 copy.260
  902.3 2.6 multiply_subtract_fusion.6
  913.0 56.4 %collective-permute-start.12 = (f32[256,128]{0,1:T(8,128)}, f32[256,128]{0,1:T(8,128)S(1)}, u32[]{:S(2)}, u32[]{:S(2)}) collective-permute-start(f32[256,128]{0,1:T(8,128)} %get-tuple-element.53), channel_id=1, source_target_pairs={{64,0},{128,64},{192,128},{0,192},{65,1},{129,65},{193,129},{1,193... | collective-permute-start | bytes 393224 | tf_op jit(solution)/shard_map/ppermute | solution.py:23
  970.8 2.3 copy.292
  974.5 2.5 collective-permute-start.13
  977.0 1.6 pad_maximum_fusion.2
  982.3 2.4 collective-permute-done.11
  989.9 1.6 slice_dynamic-update-slice_fusion.1
  994.1 12.1 fusion.9
  1011.5 1.6 collective-permute-start.17
  1013.1 4.6 collective-permute-start.15
  1021.1 1.9 collective-permute-start.18
  1023.0 1.6 pad_maximum_fusion.3
  1029.9 1.9 collective-permute-done.16
  1034.4 1.6 slice_bitcast_fusion.8
  1042.0 2.3 copy.294
  1044.3 1.9 multiply_reduce_fusion.3
  1046.2 77.9 %all-reduce.1 = (f32[128]{0:T(128)S(1)}, f32[128]{0:T(128)S(1)}) all-reduce(f32[128]{0:T(128)S(1)} %get-tuple-element.17, f32[128]{0:T(128)S(1)} %get-tuple-element.16), channel_id=1, replica_groups=mesh['clus'=4,'sub'=64] {'clus','sub'}, use_global_device_ids=true, to_apply=%region_13.16 | all-reduce | flops 256 | bytes 2048 | tf_op jit(solution)/shard_map/psum | solution.py:98
  1128.3 316.1 %psum.77 = f32[2,32,128]{2,1,0:T(8,128)S(1)} all-reduce(f32[2,32,128]{2,1,0:T(8,128)S(1)} %broadcast_multiply_fusion.1), channel_id=1, replica_groups=mesh['clus'=4,'sub'=64] {'sub'}, use_global_device_ids=true, to_apply=%region_14.17 | all-reduce | flops 8192 | bytes 65536 | tf_op jit(solution)/shard_map/psum | solution.py:86
  1448.0 2.8 multiply_subtract_fusion.2
  1456.7 56.1 %collective-permute-start.22 = (f32[256,128]{0,1:T(8,128)}, f32[256,128]{0,1:T(8,128)S(1)}, u32[]{:S(2)}, u32[]{:S(2)}) collective-permute-start(f32[256,128]{0,1:T(8,128)} %get-tuple-element.41), channel_id=1, source_target_pairs={{64,0},{128,64},{192,128},{0,192},{65,1},{129,65},{193,129},{1,193... | collective-permute-start | bytes 393224 | tf_op jit(solution)/shard_map/ppermute | solution.py:23
  1514.0 2.3 copy.329
  1517.8 2.3 collective-permute-start.23
  1524.1 3.9 collective-permute-done.21
  1528.0 1.6 bitcast_dynamic-update-slice_fusion.20
  1530.2 1.6 bitcast_dynamic-update-slice_fusion.18
  1536.6 12.4 fusion.12
  1555.6 3.3 collective-permute-start.25
  1560.5 3.7 collective-permute-start.28
  1564.2 1.7 pad_maximum_fusion.5
  1570.3 1.8 bitcast_dynamic-update-slice_fusion.5
  1575.1 1.6 bitcast_dynamic-update-slice_fusion.10
  1576.7 1.6 bitcast_dynamic-update-slice_fusion.26
  1578.3 1.6 bitcast_dynamic-update-slice_fusion.4
  1579.8 1.7 bitcast_dynamic-update-slice_fusion.3
  1581.5 1.6 bitcast_dynamic-update-slice_fusion.15
  1584.4 1.6 bitcast_dynamic-update-slice_fusion.13
  1586.0 1.6 bitcast_dynamic-update-slice_fusion.2
  1587.6 1.6 bitcast_dynamic-update-slice_fusion.8
  1589.1 1.6 bitcast_dynamic-update-slice_fusion.24
  1593.8 1.6 slice_dynamic-update-slice_fusion.3
  1595.4 1.9 multiply_reduce_fusion.1
  1597.3 76.0 %all-reduce = (f32[128]{0:T(128)S(1)}, f32[128]{0:T(128)S(1)}) all-reduce(f32[128]{0:T(128)S(1)} %get-tuple-element.15, f32[128]{0:T(128)S(1)} %get-tuple-element.14), channel_id=1, replica_groups=mesh['clus'=4,'sub'=64] {'clus','sub'}, use_global_device_ids=true, to_apply=%region_18.21 | all-reduce | flops 256 | bytes 2048 | tf_op jit(solution)/shard_map/psum | solution.py:98
  1673.2 1.7 bitcast_dynamic-update-slice_fusion.1
  1674.9 1.6 bitcast_dynamic-update-slice_fusion
  1676.5 1.6 bitcast_dynamic-update-slice_fusion.6
  1678.7 3.7 multiply_subtract_fusion
  (387 shorter events, 146.5 us)
Async XLA Ops:
  7.2 8.6 sort.19.cloned.1.call-start
  12.9 473.6 %copy-start.20 = (s32[1024]{0:T(1024)}, s32[1024]{0:T(1024)S(1)}, u32[]{:S(2)}) copy-start(s32[1024]{0:T(1024)S(1)} %pad_clamp_fusion.5) | copy-start | bytes 12292
  12.9 347.4 %copy-start.41 = (f32[2]{0:T(128)}, f32[2]{0:T(128)S(1)}, u32[]{:S(2)}) copy-start(f32[2]{0:T(128)S(1)} %compare_convert_fusion) | copy-start | bytes 28
  15.7 438.8 %copy-start.1 = (f32[1536,128]{0,1:T(8,128)}, f32[1536,128]{0,1:T(8,128)S(1)}, u32[]{:S(2)}) copy-start(f32[1536,128]{0,1:T(8,128)S(1)} %copy.224) | copy-start | bytes 2359300
  18.3 451.4 %copy-start.22 = (s32[1024]{0:T(1024)}, s32[1024]{0:T(1024)S(1)}, u32[]{:S(2)}) copy-start(s32[1024]{0:T(1024)S(1)} %pad_clamp_fusion.4) | copy-start | bytes 12292
  19.2 352.7 %copy-start.23 = (pred[256]{0:T(512)(128)(4,1)S(1)}, pred[256]{0:T(512)(128)(4,1)}, u32[]{:S(2)}) copy-start(pred[256]{0:T(512)(128)(4,1)} %get-tuple-element.87) | copy-start | bytes 772
  19.2 353.4 %copy-start.26 = (pred[256]{0:T(512)(128)(4,1)S(1)}, pred[256]{0:T(512)(128)(4,1)}, u32[]{:S(2)}) copy-start(pred[256]{0:T(512)(128)(4,1)} %get-tuple-element.86) | copy-start | bytes 772
  19.3 418.9 %copy-start.29 = (pred[256]{0:T(512)(128)(4,1)S(1)}, pred[256]{0:T(512)(128)(4,1)}, u32[]{:S(2)}) copy-start(pred[256]{0:T(512)(128)(4,1)} %get-tuple-element.85) | copy-start | bytes 772
  362.2 82.9 %copy-start.38 = (pred[256]{0:T(512)(128)(4,1)S(1)}, pred[256]{0:T(512)(128)(4,1)}, u32[]{:S(2)}) copy-start(pred[256]{0:T(512)(128)(4,1)} %compare_and_fusion.5) | copy-start | bytes 772
  362.2 85.2 %copy-start.35 = (pred[256]{0:T(512)(128)(4,1)S(1)}, pred[256]{0:T(512)(128)(4,1)}, u32[]{:S(2)}) copy-start(pred[256]{0:T(512)(128)(4,1)} %compare_and_fusion.3) | copy-start | bytes 772
  363.6 86.9 %copy-start.32 = (pred[256]{0:T(512)(128)(4,1)S(1)}, pred[256]{0:T(512)(128)(4,1)}, u32[]{:S(2)}) copy-start(pred[256]{0:T(512)(128)(4,1)} %compare_and_fusion) | copy-start | bytes 772
  372.6 73.2 %collective-permute-start.1 = (f32[256,128]{0,1:T(8,128)}, f32[256,128]{0,1:T(8,128)}, u32[]{:S(2)}, u32[]{:S(2)}) collective-permute-start(f32[256,128]{0,1:T(8,128)} %broadcast_select_fusion.11), channel_id=1, source_target_pairs={{0,1},{1,2},{2,3},{3,4},{4,5},{5,6},{6,7},{7,8},{8,9},{9,10},{10,1... | collective-permute-start | bytes 393224 | tf_op jit(solution)/shard_map/ppermute | solution.py:21
  373.3 74.7 %collective-permute-start.3 = (f32[256,128]{0,1:T(8,128)}, f32[256,128]{0,1:T(8,128)}, u32[]{:S(2)}, u32[]{:S(2)}) collective-permute-start(f32[256,128]{0,1:T(8,128)} %broadcast_select_fusion.10), channel_id=1, source_target_pairs={{0,64},{64,128},{128,192},{192,0},{1,65},{65,129},{129,193},{193,1... | collective-permute-start | bytes 393224 | tf_op jit(solution)/shard_map/ppermute | solution.py:21
  430.1 8.4 collective-permute-start.2
  430.1 13.2 collective-permute-start
  438.2 11.4 collective-permute-start.4
  451.9 15.9 copy-start.30
  453.3 15.6 copy-start.27
  454.5 26.3 %copy-start.24 = (pred[256]{0:T(512)(128)(4,1)S(1)}, pred[256]{0:T(512)(128)(4,1)}, u32[]{:S(2)}) copy-start(pred[256]{0:T(512)(128)(4,1)} %get-tuple-element.87) | copy-start | bytes 772
  470.5 14.9 collective-permute-start.7
  472.0 14.3 collective-permute-start.5
  482.8 97.2 %copy-start = (f32[1,1,32,1536]{3,2,1,0:T(8,128)S(1)}, f32[1,1,32,1536]{3,2,1,0:T(8,128)}, u32[]{:S(2)}) copy-start(f32[1,1,32,1536]{3,2,1,0:T(8,128)} %param.11) | copy-start | bytes 589828
  484.0 11.3 collective-permute-start.6
  484.0 12.0 collective-permute-start.8
  485.4 10.6 collective-permute-start.9
  486.3 9.8 copy-start.10
  487.3 8.7 copy-start.12
  497.0 407.9 %copy-start.8 = (f32[256,128]{0,1:T(8,128)}, f32[256,128]{0,1:T(8,128)S(1)}, u32[]{:S(2)}) copy-start(f32[256,128]{0,1:T(8,128)S(1)} %copy.251) | copy-start | bytes 393220
  898.8 81.0 %copy-start.21 = (s32[1024]{0:T(1024)S(1)}, s32[1024]{0:T(1024)}, u32[]{:S(2)}) copy-start(s32[1024]{0:T(1024)} %copy-done.20) | copy-start | bytes 12292
  900.0 81.4 %copy-start.39 = (pred[256]{0:T(512)(128)(4,1)S(1)}, pred[256]{0:T(512)(128)(4,1)}, u32[]{:S(2)}) copy-start(pred[256]{0:T(512)(128)(4,1)} %compare_and_fusion.5) | copy-start | bytes 772
  902.3 83.3 %copy-start.36 = (pred[256]{0:T(512)(128)(4,1)S(1)}, pred[256]{0:T(512)(128)(4,1)}, u32[]{:S(2)}) copy-start(pred[256]{0:T(512)(128)(4,1)} %compare_and_fusion.3) | copy-start | bytes 772
  902.3 87.0 %copy-start.33 = (pred[256]{0:T(512)(128)(4,1)S(1)}, pred[256]{0:T(512)(128)(4,1)}, u32[]{:S(2)}) copy-start(pred[256]{0:T(512)(128)(4,1)} %compare_and_fusion) | copy-start | bytes 772
  906.0 88.1 %copy-start.4 = (f32[1536,128]{0,1:T(8,128)S(1)}, f32[1536,128]{0,1:T(8,128)}, u32[]{:S(2)}) copy-start(f32[1536,128]{0,1:T(8,128)} %copy-done.3) | copy-start | bytes 2359300
  913.0 65.8 %collective-permute-start.12 = (f32[256,128]{0,1:T(8,128)}, f32[256,128]{0,1:T(8,128)S(1)}, u32[]{:S(2)}, u32[]{:S(2)}) collective-permute-start(f32[256,128]{0,1:T(8,128)} %get-tuple-element.53), channel_id=1, source_target_pairs={{64,0},{128,64},{192,128},{0,192},{65,1},{129,65},{193,129},{1,193... | collective-permute-start | bytes 393224 | tf_op jit(solution)/shard_map/ppermute | solution.py:23
  969.5 10.3 collective-permute-start.10
  973.0 11.6 collective-permute-start.11
  974.5 11.1 collective-permute-start.13
  978.6 8.6 collective-permute-start.14
  991.5 16.6 copy-start.31
  992.9 16.9 copy-start.28
  994.1 23.7 %copy-start.25 = (pred[256]{0:T(512)(128)(4,1)S(1)}, pred[256]{0:T(512)(128)(4,1)}, u32[]{:S(2)}) copy-start(pred[256]{0:T(512)(128)(4,1)} %get-tuple-element.87) | copy-start | bytes 772
  1011.5 13.1 collective-permute-start.17
  1013.1 13.3 collective-permute-start.15
  1021.1 10.8 collective-permute-start.16
  1021.1 12.4 collective-permute-start.18
  1024.6 9.8 collective-permute-start.19
  1039.3 411.5 %copy-start.13 = (f32[256,128]{0,1:T(8,128)}, f32[256,128]{0,1:T(8,128)S(1)}, u32[]{:S(2)}) copy-start(f32[256,128]{0,1:T(8,128)S(1)} %copy.287) | copy-start | bytes 393220
  1446.9 76.5 %copy-start.40 = (pred[256]{0:T(512)(128)(4,1)S(1)}, pred[256]{0:T(512)(128)(4,1)}, u32[]{:S(2)}) copy-start(pred[256]{0:T(512)(128)(4,1)} %compare_and_fusion.5) | copy-start | bytes 772
  1448.0 81.5 %copy-start.37 = (pred[256]{0:T(512)(128)(4,1)S(1)}, pred[256]{0:T(512)(128)(4,1)}, u32[]{:S(2)}) copy-start(pred[256]{0:T(512)(128)(4,1)} %compare_and_fusion.3) | copy-start | bytes 772
  1448.0 84.7 %copy-start.34 = (pred[256]{0:T(512)(128)(4,1)S(1)}, pred[256]{0:T(512)(128)(4,1)}, u32[]{:S(2)}) copy-start(pred[256]{0:T(512)(128)(4,1)} %compare_and_fusion) | copy-start | bytes 772
  1456.7 63.8 %collective-permute-start.22 = (f32[256,128]{0,1:T(8,128)}, f32[256,128]{0,1:T(8,128)S(1)}, u32[]{:S(2)}, u32[]{:S(2)}) collective-permute-start(f32[256,128]{0,1:T(8,128)} %get-tuple-element.41), channel_id=1, source_target_pairs={{64,0},{128,64},{192,128},{0,192},{65,1},{129,65},{193,129},{1,193... | collective-permute-start | bytes 393224 | tf_op jit(solution)/shard_map/ppermute | solution.py:23
  1512.7 8.7 collective-permute-start.20
  1516.3 11.6 collective-permute-start.21
  1517.8 12.4 collective-permute-start.23
  1520.1 11.7 collective-permute-start.24
  1549.0 30.8 %copy-start.11 = (f32[256,128]{0,1:T(8,128)S(1)}, f32[256,128]{0,1:T(8,128)}, u32[]{:S(2)}) copy-start(f32[256,128]{0,1:T(8,128)} %copy-done.10) | copy-start | bytes 393220
  1555.6 117.7 %copy-start.9 = (f32[256,128]{0,1:T(8,128)S(1)}, f32[256,128]{0,1:T(8,128)}, u32[]{:S(2)}) copy-start(f32[256,128]{0,1:T(8,128)} %copy-done.8) | copy-start | bytes 393220
  1555.6 12.7 collective-permute-start.25
  1560.4 118.3 %copy-start.7 = (f32[1,1,6,256,128]{3,4,2,1,0:T(8,128)S(1)}, f32[1,1,6,256,128]{3,4,2,1,0:T(8,128)}, u32[]{:S(2)}) copy-start(f32[1,1,6,256,128]{3,4,2,1,0:T(8,128)} %copy.254) | copy-start | bytes 2359300
  1560.4 17.8 %collective-permute-start.26 = (f32[256,128]{0,1:T(8,128)}, f32[256,128]{0,1:T(8,128)}, u32[]{:S(2)}, u32[]{:S(2)}) collective-permute-start(f32[256,128]{0,1:T(8,128)} %broadcast_select_fusion.1), channel_id=1, source_target_pairs={{0,1},{1,2},{2,3},{3,4},{4,5},{5,6},{6,7},{7,8},{8,9},{9,10},{10,1... | collective-permute-start | bytes 393224 | tf_op jit(solution)/shard_map/ppermute | solution.py:21
  1560.5 23.9 %collective-permute-start.28 = (f32[256,128]{0,1:T(8,128)}, f32[256,128]{0,1:T(8,128)}, u32[]{:S(2)}, u32[]{:S(2)}) collective-permute-start(f32[256,128]{0,1:T(8,128)} %broadcast_select_fusion), channel_id=1, source_target_pairs={{0,64},{64,128},{128,192},{192,0},{1,65},{65,129},{129,193},{193,1... | collective-permute-start | bytes 393224 | tf_op jit(solution)/shard_map/ppermute | solution.py:21
  1564.2 9.1 collective-permute-start.27
  1565.9 24.8 %collective-permute-start.29 = (f32[2,256,128]{1,2,0:T(8,128)}, f32[2,256,128]{1,2,0:T(8,128)}, u32[]{:S(2)}, u32[]{:S(2)}) collective-permute-start(f32[2,256,128]{1,2,0:T(8,128)} %pad_maximum_fusion.5), channel_id=1, source_target_pairs={{0,32},{1,33},{2,34},{3,35},{4,36},{5,37},{6,38},{7,39},{8,40},{9,... | collective-permute-start | bytes 786440 | tf_op jit(solution)/shard_map/ppermute | solution.py:31
  1568.3 109.8 %copy-start.17 = (f32[2,256,128]{1,2,0:T(8,128)S(1)}, f32[2,256,128]{1,2,0:T(8,128)}, u32[]{:S(2)}) copy-start(f32[2,256,128]{1,2,0:T(8,128)} %copy-done.16) | copy-start | bytes 786436
  (11 other events, 19.7 us)
Sparse Core Ops, SparseCore 0:
  10.9 2.5 sort.21.cloned.1.call-done
  (1 shorter events, 0.0 us)
where the time goes:
time: 1700 us; the launch traced here: 1690 us
  blocking collectives  1190 us (70%)
  starting transfers between devices  212 us (12%)
  local copies, waits for them, and re-layouts  131 us (8%)
  other arithmetic  76 us (4%)
  matrix products  45.8 us (3%)
  waiting for transfers between devices  20.2 us (1%)
    psum x3, blocking collectives, per_device(): gathered = lax.psum(selector[:, None, None] * projected[None], 'sub')  959 us
    psum x3, blocking collectives, per_device(): lax.psum((jnp.sum(residual * search, axis=(0, 1)), jnp.sum(search * assem...  231 us
    ppermute x12, starting transfers between devices, with_halo(): lax.ppermute(head, axis, [((i + 1) % count, i) for i in range(count)])  140 us
    ppermute x12, starting transfers between devices, with_halo(): lax.ppermute(tail, axis, [(i, (i + 1) % count) for i in range(count)])  70.9 us
    dot_general x3, matrix products, per_device(): jnp.dot(operator, local_copy.reshape(ORDER, COLS), precision=highest)  36.7 us
  transfers between devices with their start and end apart: 30, of which 6 were waited for; matrix products, arithmetic and copies ran while one was open for 5% of the time, Pallas kernels for 0%

commit v1 on v0

--- a/solution.py
+++ b/solution.py
@@ -83,7 +83,8 @@
         projected = jnp.einsum(
             "mn,nc->mc", mode_rows, residual.reshape(ORDER, COLS), precision=highest
         )
-        gathered = lax.psum(selector[:, None, None] * projected[None], "sub")
+        z_in = selector[:, None, None] * projected[None]
+        gathered = jnp.sum(lax.all_gather(z_in, axis_name="sub"), 0)
         coefficients = jax.vmap(solve_one)(factor, gathered)
         own_coeff = lax.dynamic_index_in_dim(coefficients, member, 0, keepdims=False)
         correction = jnp.einsum("mn,mc->nc", mode_rows, own_coeff, precision=highest).reshape(

time: 1700 us -> 1130 us (0.66)
  blocking collectives: 1190 us -> 557 us
  waiting for transfers between devices: 20.2 us -> 160 us
  starting transfers between devices: 212 us -> 109 us
    psum x3 -> x1, blocking collectives: 959 us -> 328 us  [per_device(): gram_total = lax.psum(selector[:, None, None] * gram_terms[None], 'sub')]
    all_gather x0 -> x3, waiting for transfers between devices: none -> 133 us  [per_device(): gathered = jnp.sum(lax.all_gather(z_in, axis_name='sub'), 0)]
    ppermute x12, starting transfers between devices: 140 us -> 43.5 us  [with_halo(): lax.ppermute(head, axis, [((i + 1) % count, i) for i in range(count)])]
  transfers between devices with their start and end apart: 30 -> 33, of which waited for: 6 -> 7; matrix products, arithmetic and copies ran while one was open for 5% -> 9% of each run, Pallas kernels for 0% -> 0%
where the time goes in v1:
time: 1130 us; the launch traced here: 1120 us
  blocking collectives  557 us (49%)
  waiting for transfers between devices  160 us (14%)
  local copies, waits for them, and re-layouts  144 us (13%)
  starting transfers between devices  109 us (10%)
  other arithmetic  85.8 us (8%)
  matrix products  45.8 us (4%)
  between operations  16.4 us (1%)
    psum x1, blocking collectives, per_device(): gram_total = lax.psum(selector[:, None, None] * gram_terms[None], 'sub')  328 us
    psum x3, blocking collectives, per_device(): lax.psum((jnp.sum(residual * search, axis=(0, 1)), jnp.sum(search * assem...  229 us
    all_gather x3, waiting for transfers between devices, per_device(): gathered = jnp.sum(lax.all_gather(z_in, axis_name='sub'), 0)  133 us
    ppermute x12, starting transfers between devices, with_halo(): lax.ppermute(tail, axis, [(i, (i + 1) % count) for i in range(count)])  63.4 us
    ppermute x12, starting transfers between devices, with_halo(): lax.ppermute(head, axis, [((i + 1) % count, i) for i in range(count)])  43.5 us
    dot_general x3, matrix products, per_device(): jnp.dot(operator, local_copy.reshape(ORDER, COLS), precision=highest)  36.7 us
    unnamed x99, local copies, waits for them, and re-layouts  32.3 us
    ppermute x12, waiting for transfers between devices, with_halo(): lax.ppermute(tail, axis, [(i, (i + 1) % count) for i in range(count)])  23.5 us
  transfers between devices with their start and end apart: 33, of which 7 were waited for; matrix products, arithmetic and copies ran while one was open for 9% of the time, Pallas kernels for 0%

profile of v1, /device:TPU:1, one launch (start us, length us, event | category | flops | bytes accessed | tf_op | source)
XLA Modules:
  0.0 1117.8 jit_solution(14273130519415006041)
XLA Ops:
  21.2 327.7 %psum.49 = f32[2,32,32]{1,2,0:T(8,128)S(1)} all-reduce(f32[2,32,32]{1,2,0:T(8,128)S(1)} %broadcast_multiply_fusion.4), channel_id=1, replica_groups=mesh['clus'=4,'sub'=64] {'sub'}, use_global_device_ids=true, to_apply=%region_0.0 | all-reduce | flops 2048 | bytes 16384 | tf_op jit(solution)/shard_map/psum | solution.py:78
  349.1 5.9 custom-call.9
  355.2 4.9 custom-call.12
  360.7 1.7 reduce_sum.81
  374.7 56.4 %collective-permute-start.3 = (f32[256,128]{0,1:T(8,128)}, f32[256,128]{0,1:T(8,128)}, u32[]{:S(2)}, u32[]{:S(2)}) collective-permute-start(f32[256,128]{0,1:T(8,128)} %broadcast_select_fusion.10), channel_id=1, source_target_pairs={{0,64},{64,128},{128,192},{192,0},{1,65},{65,129},{129,193},{193,1... | collective-permute-start | bytes 393224 | tf_op jit(solution)/shard_map/ppermute | solution.py:21
  431.1 8.1 collective-permute-start
  442.9 2.5 collective-permute-done
  455.9 12.2 %fusion.6 = f32[1536,128]{0,1:T(8,128)S(1)} fusion(f32[1,1,1536,1536]{3,2,1,0:T(8,128)} %param.10, f32[1536,128]{0,1:T(8,128)S(1)} %copy.357, f32[1536,128]{0,1:T(8,128)} %copy-done.10, f32[1536,128]{0,1:T(8,128)S(1)} %copy.343, f32[1536]{0:T(1024)S(1)} %broadcast_subtract_fusion, f32[1536]{0:T(1024)S(1)} %reshape.635), kind=kOutput, calls=%fused_computation.45 | convolution fusion | flops 3624861696 | bytes 12595200 | tf_op jit(solution)/shard_map/dot_general | solution.py:95
  472.2 8.6 collective-permute-start.5
  487.6 6.7 collective-permute-done.6
  500.5 2.2 multiply_reduce_fusion.5
  503.8 76.3 %all-reduce.2 = (f32[128]{0:T(128)S(1)}, f32[128]{0:T(128)S(1)}) all-reduce(f32[128]{0:T(128)} %get-tuple-element.15, f32[128]{0:T(128)} %get-tuple-element.14), channel_id=1, replica_groups=mesh['clus'=4,'sub'=64] {'clus','sub'}, use_global_device_ids=true, to_apply=%region_8.11 | all-reduce | flops 256 | bytes 2048 | tf_op jit(solution)/shard_map/psum | solution.py:99
  580.1 1.6 multiply_subtract_fusion.7
  583.9 71.1 %all-gather.6.cloned.1.call-done = f32[64,2,32,128]{3,2,1,0:T(8,128)} async-done(((f32[1,2,32,128]{3,2,1,0:T(8,128)}), f32[64,2,32,128]{3,2,1,0:T(8,128)}) %all-gather.6.cloned.1.call-update) | async-done | bytes 2097168 | tf_op jit(solution)/shard_map/all_gather | solution.py:87
  655.0 1.7 reduce_sum.84
  657.2 1.7 convolution_bitcast_fusion.1
  661.4 2.5 multiply_subtract_fusion.6
  671.6 3.1 collective-permute-start.12
  674.7 6.0 collective-permute-start.10
  682.3 1.6 pad_maximum_fusion.2
  688.1 5.7 collective-permute-done.11
  704.4 12.1 %fusion.9 = f32[1536,128]{0,1:T(8,128)S(1)} fusion(f32[1,1,1536,1536]{3,2,1,0:T(8,128)} %param.10, f32[1536,128]{0,1:T(8,128)} %copy.393, f32[1536,128]{0,1:T(8,128)S(1)} %multiply_subtract_fusion.7, f32[1536,128]{0,1:T(8,128)S(1)} %copy-done.9, f32[1536]{0:T(1024)S(1)} %broadcast_subtract_fusion, f32[1536]{0:T(1024)S(1)} %reshape.635), kind=kOutput, calls=%fused_computation.46 | convolution fusion | flops 3624665088 | bytes 12595200 | tf_op jit(solution)/shard_map/dot_general | solution.py:95
  722.7 2.2 collective-permute-start.17
  724.9 3.4 collective-permute-start.15
  732.1 1.6 pad_maximum_fusion.3
  739.1 3.9 collective-permute-done.16
  745.5 1.6 slice_bitcast_fusion.8
  753.2 2.3 copy.413
  755.4 2.4 multiply_reduce_fusion.3
  757.8 76.0 %all-reduce.1 = (f32[128]{0:T(128)}, f32[128]{0:T(128)}) all-reduce(f32[128]{0:T(128)} %get-tuple-element.19, f32[128]{0:T(128)} %get-tuple-element.18), channel_id=1, replica_groups=mesh['clus'=4,'sub'=64] {'clus','sub'}, use_global_device_ids=true, to_apply=%region_13.16 | all-reduce | flops 256 | bytes 2048 | tf_op jit(solution)/shard_map/psum | solution.py:99
  838.9 2.3 copy.373
  841.1 2.3 copy.409
  843.4 2.3 copy.411
  845.7 2.3 copy.446
  848.0 62.2 %all-gather.8.cloned.1.call-done = f32[64,2,32,128]{3,2,1,0:T(8,128)} async-done(((f32[1,2,32,128]{3,2,1,0:T(8,128)}), f32[64,2,32,128]{3,2,1,0:T(8,128)}) %all-gather.8.cloned.1.call-update) | async-done | bytes 2097168 | tf_op jit(solution)/shard_map/all_gather | solution.py:87
  910.3 1.7 reduce_sum.87
  914.4 2.3 copy.416
  916.7 2.5 multiply_subtract_fusion.2
  924.8 3.1 collective-permute-start.22
  927.9 6.0 collective-permute-start.20
  935.3 2.3 copy.448
  942.1 7.2 collective-permute-done.21
  949.3 1.6 bitcast_dynamic-update-slice_fusion.20
  951.5 1.6 bitcast_dynamic-update-slice_fusion.18
  958.0 12.4 %fusion.12 = f32[1536,128]{0,1:T(8,128)S(1)} fusion(f32[1,1,1536,1536]{3,2,1,0:T(8,128)} %param.10, f32[1536,128]{0,1:T(8,128)} %copy.430, f32[1536,128]{0,1:T(8,128)} %copy-done.12, f32[1536,128]{0,1:T(8,128)S(1)} %copy-done.8, f32[1536]{0:T(1024)S(1)} %broadcast_subtract_fusion, f32[1536]{0:T(1024)S(1)} %reshape.635), kind=kOutput, calls=%fused_computation.47 | convolution fusion | flops 3624665088 | bytes 12595200 | tf_op jit(solution)/shard_map/dot_general | solution.py:95
  975.2 2.3 collective-permute-start.25
  978.6 4.0 collective-permute-start.28
  982.6 1.7 pad_maximum_fusion.5
  990.1 1.7 bitcast_dynamic-update-slice_fusion.5
  995.8 1.6 bitcast_dynamic-update-slice_fusion.10
  1000.5 1.7 bitcast_dynamic-update-slice_fusion.3
  1002.2 1.6 bitcast_dynamic-update-slice_fusion.15
  1004.4 1.6 bitcast_dynamic-update-slice_fusion.13
  1006.0 1.6 bitcast_dynamic-update-slice_fusion.2
  1007.6 1.6 bitcast_dynamic-update-slice_fusion.8
  1010.7 1.6 slice_bitcast_fusion
  1017.8 1.9 multiply_reduce_fusion.1
  1019.7 76.9 %all-reduce = (f32[128]{0:T(128)S(1)}, f32[128]{0:T(128)S(1)}) all-reduce(f32[128]{0:T(128)S(1)} %get-tuple-element.17, f32[128]{0:T(128)S(1)} %get-tuple-element.16), channel_id=1, replica_groups=mesh['clus'=4,'sub'=64] {'clus','sub'}, use_global_device_ids=true, to_apply=%region_18.21 | all-reduce | flops 256 | bytes 2048 | tf_op jit(solution)/shard_map/psum | solution.py:99
  1096.6 1.7 bitcast_dynamic-update-slice_fusion.1
  1098.3 1.6 bitcast_dynamic-update-slice_fusion
  1099.9 1.6 bitcast_dynamic-update-slice_fusion.6
  1101.4 1.6 bitcast_dynamic-update-slice_fusion.22
  1103.0 4.3 multiply_subtract_fusion
  1107.4 2.3 copy.452
  (385 shorter events, 162.7 us)
Async XLA Ops:
  7.2 355.7 %copy-start = (f32[1,1,32,1536]{3,2,1,0:T(8,128)S(1)}, f32[1,1,32,1536]{3,2,1,0:T(8,128)}, u32[]{:S(2)}) copy-start(f32[1,1,32,1536]{3,2,1,0:T(8,128)} %param.11) | copy-start | bytes 589828
  7.2 7.0 sort.19.cloned.1.call-start
  9.2 351.6 %all-gather.4.cloned.1.call-start = ((), (), s32[]{:S(2)}) async-start(), calls=%async_computation | async-start | bytes 2129920 | tf_op jit(solution)/shard_map/all_gather | solution.py:87
  11.3 9.9 copy-start.33
  14.1 441.7 %copy-start.3 = (f32[1536,128]{0,1:T(8,128)}, f32[1536,128]{0,1:T(8,128)S(1)}, u32[]{:S(2)}) copy-start(f32[1536,128]{0,1:T(8,128)S(1)} %copy.343) | copy-start | bytes 2359300
  18.1 636.9 %all-gather.6.cloned.1.call-start = ((), (), s32[]{:S(2)}) async-start(), calls=%async_computation.1 | async-start | bytes 2129920 | tf_op jit(solution)/shard_map/all_gather | solution.py:87
  363.7 88.4 %copy-start.10 = (f32[1536,128]{0,1:T(8,128)}, f32[1536,128]{0,1:T(8,128)S(1)}, u32[]{:S(2)}) copy-start(f32[1536,128]{0,1:T(8,128)S(1)} %convolution_bitcast_fusion.2) | copy-start | bytes 2359300
  364.0 3.3 copy-start.1
  373.5 74.5 %collective-permute-start.1 = (f32[256,128]{0,1:T(8,128)}, f32[256,128]{0,1:T(8,128)}, u32[]{:S(2)}, u32[]{:S(2)}) collective-permute-start(f32[256,128]{0,1:T(8,128)} %broadcast_select_fusion.11), channel_id=1, source_target_pairs={{0,1},{1,2},{2,3},{3,4},{4,5},{5,6},{6,7},{7,8},{8,9},{9,10},{10,1... | collective-permute-start | bytes 393224 | tf_op jit(solution)/shard_map/ppermute | solution.py:21
  374.7 74.8 %collective-permute-start.3 = (f32[256,128]{0,1:T(8,128)}, f32[256,128]{0,1:T(8,128)}, u32[]{:S(2)}, u32[]{:S(2)}) collective-permute-start(f32[256,128]{0,1:T(8,128)} %broadcast_select_fusion.10), channel_id=1, source_target_pairs={{0,64},{64,128},{128,192},{192,0},{1,65},{65,129},{129,193},{193,1... | collective-permute-start | bytes 393224 | tf_op jit(solution)/shard_map/ppermute | solution.py:21
  431.1 10.0 collective-permute-start.2
  431.1 14.3 %collective-permute-start = (f32[256,128]{0,1:T(8,128)}, f32[256,128]{0,1:T(8,128)}, u32[]{:S(2)}, u32[]{:S(2)}) collective-permute-start(f32[256,128]{0,1:T(8,128)} %get-tuple-element.67), channel_id=1, source_target_pairs={{1,0},{2,1},{3,2},{4,3},{5,4},{6,5},{7,6},{8,7},{9,8},{10,9},{11,1... | collective-permute-start | bytes 393224 | tf_op jit(solution)/shard_map/ppermute | solution.py:23
  440.8 9.7 collective-permute-start.4
  454.2 14.9 %copy-start.28 = (pred[256]{0:T(512)(128)(4,1)S(1)}, pred[256]{0:T(512)(128)(4,1)}, u32[]{:S(2)}) copy-start(pred[256]{0:T(512)(128)(4,1)} %get-tuple-element.85) | copy-start | bytes 772
  455.6 14.5 %copy-start.26 = (pred[256]{0:T(512)(128)(4,1)S(1)}, pred[256]{0:T(512)(128)(4,1)}, u32[]{:S(2)}) copy-start(pred[256]{0:T(512)(128)(4,1)} %get-tuple-element.86) | copy-start | bytes 772
  455.9 25.0 %copy-start.24 = (pred[256]{0:T(512)(128)(4,1)S(1)}, pred[256]{0:T(512)(128)(4,1)}, u32[]{:S(2)}) copy-start(pred[256]{0:T(512)(128)(4,1)} %get-tuple-element.87) | copy-start | bytes 772
  471.7 13.5 %collective-permute-start.7 = (f32[256,128]{0,1:T(8,128)S(1)}, f32[256,128]{0,1:T(8,128)S(1)}, u32[]{:S(2)}, u32[]{:S(2)}) collective-permute-start(f32[256,128]{0,1:T(8,128)S(1)} %get-tuple-element.59), channel_id=1, source_target_pairs={{64,0},{128,64},{192,128},{0,192},{65,1},{129,65},{193,129},{1,193... | collective-permute-start | bytes 393224 | tf_op jit(solution)/shard_map/ppermute | solution.py:23
  472.2 13.8 %collective-permute-start.5 = (f32[256,128]{0,1:T(8,128)S(1)}, f32[256,128]{0,1:T(8,128)S(1)}, u32[]{:S(2)}, u32[]{:S(2)}) collective-permute-start(f32[256,128]{0,1:T(8,128)S(1)} %get-tuple-element.61), channel_id=1, source_target_pairs={{1,0},{2,1},{3,2},{4,3},{5,4},{6,5},{7,6},{8,7},{9,8},{10,9},{11,1... | collective-permute-start | bytes 393224 | tf_op jit(solution)/shard_map/ppermute | solution.py:23
  481.8 3.3 copy-start.2
  483.0 11.3 %collective-permute-start.6 = (f32[256,128]{0,1:T(8,128)}, f32[256,128]{0,1:T(8,128)}, u32[]{:S(2)}, u32[]{:S(2)}) collective-permute-start(f32[256,128]{0,1:T(8,128)} %broadcast_select_fusion.9), channel_id=1, source_target_pairs={{0,1},{1,2},{2,3},{3,4},{4,5},{5,6},{6,7},{7,8},{8,9},{9,10},{10,1... | collective-permute-start | bytes 393224 | tf_op jit(solution)/shard_map/ppermute | solution.py:21
  483.0 12.9 %collective-permute-start.8 = (f32[256,128]{0,1:T(8,128)}, f32[256,128]{0,1:T(8,128)}, u32[]{:S(2)}, u32[]{:S(2)}) collective-permute-start(f32[256,128]{0,1:T(8,128)} %broadcast_select_fusion.8), channel_id=1, source_target_pairs={{0,64},{64,128},{128,192},{192,0},{1,65},{65,129},{129,193},{193,1... | collective-permute-start | bytes 393224 | tf_op jit(solution)/shard_map/ppermute | solution.py:21
  485.1 11.7 %collective-permute-start.9 = (f32[2,256,128]{1,2,0:T(8,128)}, f32[2,256,128]{1,2,0:T(8,128)}, u32[]{:S(2)}, u32[]{:S(2)}) collective-permute-start(f32[2,256,128]{1,2,0:T(8,128)} %pad_maximum_fusion.1), channel_id=1, source_target_pairs={{0,32},{1,33},{2,34},{3,35},{4,36},{5,37},{6,38},{7,39},{8,40},{9,... | collective-permute-start | bytes 786440 | tf_op jit(solution)/shard_map/ppermute | solution.py:31
  486.1 11.7 %copy-start.18 = (f32[256,128]{0,1:T(8,128)}, f32[256,128]{0,1:T(8,128)S(1)}, u32[]{:S(2)}) copy-start(f32[256,128]{0,1:T(8,128)S(1)} %copy.364) | copy-start | bytes 393220
  487.0 9.8 copy-start.19
  498.6 165.3 %copy-start.16 = (f32[256,128]{0,1:T(8,128)}, f32[256,128]{0,1:T(8,128)S(1)}, u32[]{:S(2)}) copy-start(f32[256,128]{0,1:T(8,128)S(1)} %copy.370) | copy-start | bytes 393220
  583.8 326.4 %all-gather.8.cloned.1.call-start = ((), (), s32[]{:S(2)}) async-start(), calls=%async_computation.2 | async-start | bytes 2129920 | tf_op jit(solution)/shard_map/all_gather | solution.py:87
  660.3 4.6 copy-start.5
  664.0 40.5 %copy-start.9 = (f32[1536,128]{0,1:T(8,128)S(1)}, f32[1536,128]{0,1:T(8,128)}, u32[]{:S(2)}) copy-start(f32[1536,128]{0,1:T(8,128)} %convolution_bitcast_fusion.1) | copy-start | bytes 2359300
  671.6 13.0 %collective-permute-start.12 = (f32[256,128]{0,1:T(8,128)}, f32[256,128]{0,1:T(8,128)S(1)}, u32[]{:S(2)}, u32[]{:S(2)}) collective-permute-start(f32[256,128]{0,1:T(8,128)} %get-tuple-element.53), channel_id=1, source_target_pairs={{64,0},{128,64},{192,128},{0,192},{65,1},{129,65},{193,129},{1,193... | collective-permute-start | bytes 393224 | tf_op jit(solution)/shard_map/ppermute | solution.py:23
  674.7 10.8 collective-permute-start.10
  682.1 11.7 %collective-permute-start.11 = (f32[256,128]{0,1:T(8,128)}, f32[256,128]{0,1:T(8,128)}, u32[]{:S(2)}, u32[]{:S(2)}) collective-permute-start(f32[256,128]{0,1:T(8,128)} %broadcast_select_fusion.7), channel_id=1, source_target_pairs={{0,1},{1,2},{2,3},{3,4},{4,5},{5,6},{6,7},{7,8},{8,9},{9,10},{10,1... | collective-permute-start | bytes 393224 | tf_op jit(solution)/shard_map/ppermute | solution.py:21
  682.1 13.3 %collective-permute-start.13 = (f32[256,128]{0,1:T(8,128)}, f32[256,128]{0,1:T(8,128)}, u32[]{:S(2)}, u32[]{:S(2)}) collective-permute-start(f32[256,128]{0,1:T(8,128)} %broadcast_select_fusion.6), channel_id=1, source_target_pairs={{0,64},{64,128},{128,192},{192,0},{1,65},{65,129},{129,193},{193,1... | collective-permute-start | bytes 393224 | tf_op jit(solution)/shard_map/ppermute | solution.py:21
  683.9 12.4 %collective-permute-start.14 = (f32[2,256,128]{1,2,0:T(8,128)}, f32[2,256,128]{1,2,0:T(8,128)}, u32[]{:S(2)}, u32[]{:S(2)}) collective-permute-start(f32[2,256,128]{1,2,0:T(8,128)} %pad_maximum_fusion.2), channel_id=1, source_target_pairs={{0,32},{1,33},{2,34},{3,35},{4,36},{5,37},{6,38},{7,39},{8,40},{9,... | collective-permute-start | bytes 786440 | tf_op jit(solution)/shard_map/ppermute | solution.py:31
  722.7 11.1 collective-permute-start.17
  724.9 10.7 collective-permute-start.15
  729.8 3.9 copy-start.11
  731.1 12.0 %collective-permute-start.16 = (f32[256,128]{0,1:T(8,128)}, f32[256,128]{0,1:T(8,128)}, u32[]{:S(2)}, u32[]{:S(2)}) collective-permute-start(f32[256,128]{0,1:T(8,128)} %broadcast_select_fusion.5), channel_id=1, source_target_pairs={{0,1},{1,2},{2,3},{3,4},{4,5},{5,6},{6,7},{7,8},{8,9},{9,10},{10,1... | collective-permute-start | bytes 393224 | tf_op jit(solution)/shard_map/ppermute | solution.py:21
  731.1 13.5 %collective-permute-start.18 = (f32[256,128]{0,1:T(8,128)}, f32[256,128]{0,1:T(8,128)}, u32[]{:S(2)}, u32[]{:S(2)}) collective-permute-start(f32[256,128]{0,1:T(8,128)} %broadcast_select_fusion.4), channel_id=1, source_target_pairs={{0,64},{64,128},{128,192},{192,0},{1,65},{65,129},{129,193},{193,1... | collective-permute-start | bytes 393224 | tf_op jit(solution)/shard_map/ppermute | solution.py:21
  733.8 11.7 %collective-permute-start.19 = (f32[2,256,128]{1,2,0:T(8,128)}, f32[2,256,128]{1,2,0:T(8,128)}, u32[]{:S(2)}, u32[]{:S(2)}) collective-permute-start(f32[2,256,128]{1,2,0:T(8,128)} %pad_maximum_fusion.3), channel_id=1, source_target_pairs={{0,32},{1,33},{2,34},{3,35},{4,36},{5,37},{6,38},{7,39},{8,40},{9,... | collective-permute-start | bytes 786440 | tf_op jit(solution)/shard_map/ppermute | solution.py:31
  735.6 9.9 copy-start.21
  750.5 161.5 %copy-start.20 = (f32[256,128]{0,1:T(8,128)}, f32[256,128]{0,1:T(8,128)S(1)}, u32[]{:S(2)}) copy-start(f32[256,128]{0,1:T(8,128)S(1)} %copy.406) | copy-start | bytes 393220
  836.7 80.0 %copy-start.4 = (f32[6,256,128]{1,2,0:T(8,128)S(1)}, f32[6,256,128]{1,2,0:T(8,128)}, u32[]{:S(2)}) copy-start(f32[6,256,128]{1,2,0:T(8,128)} %get-tuple-element.29) | copy-start | bytes 2359300
  914.4 27.0 %copy-start.32 = (pred[256]{0:T(512)(128)(4,1)S(1)}, pred[256]{0:T(512)(128)(4,1)}, u32[]{:S(2)}) copy-start(pred[256]{0:T(512)(128)(4,1)} %compare_and_fusion.5) | copy-start | bytes 772
  916.7 34.1 %copy-start.31 = (pred[256]{0:T(512)(128)(4,1)S(1)}, pred[256]{0:T(512)(128)(4,1)}, u32[]{:S(2)}) copy-start(pred[256]{0:T(512)(128)(4,1)} %compare_and_fusion.3) | copy-start | bytes 772
  916.7 37.3 %copy-start.30 = (pred[256]{0:T(512)(128)(4,1)S(1)}, pred[256]{0:T(512)(128)(4,1)}, u32[]{:S(2)}) copy-start(pred[256]{0:T(512)(128)(4,1)} %compare_and_fusion) | copy-start | bytes 772
  920.0 37.9 %copy-start.8 = (f32[1536,128]{0,1:T(8,128)S(1)}, f32[1536,128]{0,1:T(8,128)}, u32[]{:S(2)}) copy-start(f32[1536,128]{0,1:T(8,128)} %copy-done.7) | copy-start | bytes 2359300
  924.8 13.9 %collective-permute-start.22 = (f32[256,128]{0,1:T(8,128)}, f32[256,128]{0,1:T(8,128)S(1)}, u32[]{:S(2)}, u32[]{:S(2)}) collective-permute-start(f32[256,128]{0,1:T(8,128)} %get-tuple-element.41), channel_id=1, source_target_pairs={{64,0},{128,64},{192,128},{0,192},{65,1},{129,65},{193,129},{1,193... | collective-permute-start | bytes 393224 | tf_op jit(solution)/shard_map/ppermute | solution.py:23
  927.9 11.7 %collective-permute-start.20 = (f32[256,128]{0,1:T(8,128)}, f32[256,128]{0,1:T(8,128)}, u32[]{:S(2)}, u32[]{:S(2)}) collective-permute-start(f32[256,128]{0,1:T(8,128)} %get-tuple-element.43), channel_id=1, source_target_pairs={{1,0},{2,1},{3,2},{4,3},{5,4},{6,5},{7,6},{8,7},{9,8},{10,9},{11,1... | collective-permute-start | bytes 393224 | tf_op jit(solution)/shard_map/ppermute | solution.py:23
  937.6 11.7 %collective-permute-start.21 = (f32[256,128]{0,1:T(8,128)}, f32[256,128]{0,1:T(8,128)}, u32[]{:S(2)}, u32[]{:S(2)}) collective-permute-start(f32[256,128]{0,1:T(8,128)} %broadcast_select_fusion.3), channel_id=1, source_target_pairs={{0,1},{1,2},{2,3},{3,4},{4,5},{5,6},{6,7},{7,8},{8,9},{9,10},{10,1... | collective-permute-start | bytes 393224 | tf_op jit(solution)/shard_map/ppermute | solution.py:21
  937.6 14.0 %collective-permute-start.23 = (f32[256,128]{0,1:T(8,128)}, f32[256,128]{0,1:T(8,128)}, u32[]{:S(2)}, u32[]{:S(2)}) collective-permute-start(f32[256,128]{0,1:T(8,128)} %broadcast_select_fusion.2), channel_id=1, source_target_pairs={{0,64},{64,128},{128,192},{192,0},{1,65},{65,129},{129,193},{193,1... | collective-permute-start | bytes 393224 | tf_op jit(solution)/shard_map/ppermute | solution.py:21
  937.8 15.3 %collective-permute-start.24 = (f32[2,256,128]{1,2,0:T(8,128)S(1)}, f32[2,256,128]{1,2,0:T(8,128)S(1)}, u32[]{:S(2)}, u32[]{:S(2)}) collective-permute-start(f32[2,256,128]{1,2,0:T(8,128)S(1)} %pad_maximum_fusion.4), channel_id=1, source_target_pairs={{0,32},{1,33},{2,34},{3,35},{4,36},{5,37},{6,38},{7,39},{8,40},{9,... | collective-permute-start | bytes 786440 | tf_op jit(solution)/shard_map/ppermute | solution.py:31
  955.4 16.6 %copy-start.29 = (pred[256]{0:T(512)(128)(4,1)S(1)}, pred[256]{0:T(512)(128)(4,1)}, u32[]{:S(2)}) copy-start(pred[256]{0:T(512)(128)(4,1)} %get-tuple-element.85) | copy-start | bytes 772
  956.8 16.8 %copy-start.27 = (pred[256]{0:T(512)(128)(4,1)S(1)}, pred[256]{0:T(512)(128)(4,1)}, u32[]{:S(2)}) copy-start(pred[256]{0:T(512)(128)(4,1)} %get-tuple-element.86) | copy-start | bytes 772
  958.0 19.6 %copy-start.25 = (pred[256]{0:T(512)(128)(4,1)S(1)}, pred[256]{0:T(512)(128)(4,1)}, u32[]{:S(2)}) copy-start(pred[256]{0:T(512)(128)(4,1)} %get-tuple-element.87) | copy-start | bytes 772
  975.2 121.4 %copy-start.17 = (f32[256,128]{0,1:T(8,128)S(1)}, f32[256,128]{0,1:T(8,128)}, u32[]{:S(2)}) copy-start(f32[256,128]{0,1:T(8,128)} %copy-done.16) | copy-start | bytes 393220
  975.2 11.4 %collective-permute-start.25 = (f32[256,128]{0,1:T(8,128)}, f32[256,128]{0,1:T(8,128)}, u32[]{:S(2)}, u32[]{:S(2)}) collective-permute-start(f32[256,128]{0,1:T(8,128)} %get-tuple-element.37), channel_id=1, source_target_pairs={{1,0},{2,1},{3,2},{4,3},{5,4},{6,5},{7,6},{8,7},{9,8},{10,9},{11,1... | collective-permute-start | bytes 393224 | tf_op jit(solution)/shard_map/ppermute | solution.py:23
  978.5 124.5 %copy-start.14 = (f32[1,1,6,256,128]{3,4,2,1,0:T(8,128)S(1)}, f32[1,1,6,256,128]{3,4,2,1,0:T(8,128)}, u32[]{:S(2)}) copy-start(f32[1,1,6,256,128]{3,4,2,1,0:T(8,128)} %copy.373) | copy-start | bytes 2359300
  978.5 124.5 %copy-start.35 = (f32[128]{0:T(128)S(1)}, f32[128]{0:T(128)}, u32[]{:S(2)}) copy-start(f32[128]{0:T(128)} %copy-done.34) | copy-start | bytes 1540
  978.5 124.5 %copy-start.37 = (f32[128]{0:T(128)S(1)}, f32[128]{0:T(128)}, u32[]{:S(2)}) copy-start(f32[128]{0:T(128)} %copy-done.36) | copy-start | bytes 1540
  978.5 20.4 %collective-permute-start.26 = (f32[256,128]{0,1:T(8,128)}, f32[256,128]{0,1:T(8,128)}, u32[]{:S(2)}, u32[]{:S(2)}) collective-permute-start(f32[256,128]{0,1:T(8,128)} %broadcast_select_fusion.1), channel_id=1, source_target_pairs={{0,1},{1,2},{2,3},{3,4},{4,5},{5,6},{6,7},{7,8},{8,9},{9,10},{10,1... | collective-permute-start | bytes 393224 | tf_op jit(solution)/shard_map/ppermute | solution.py:21
  978.6 25.8 %collective-permute-start.28 = (f32[256,128]{0,1:T(8,128)}, f32[256,128]{0,1:T(8,128)}, u32[]{:S(2)}, u32[]{:S(2)}) collective-permute-start(f32[256,128]{0,1:T(8,128)} %broadcast_select_fusion), channel_id=1, source_target_pairs={{0,64},{64,128},{128,192},{192,0},{1,65},{65,129},{129,193},{193,1... | collective-permute-start | bytes 393224 | tf_op jit(solution)/shard_map/ppermute | solution.py:21
  982.6 9.8 collective-permute-start.27
  984.3 26.3 %collective-permute-start.29 = (f32[2,256,128]{1,2,0:T(8,128)}, f32[2,256,128]{1,2,0:T(8,128)}, u32[]{:S(2)}, u32[]{:S(2)}) collective-permute-start(f32[2,256,128]{1,2,0:T(8,128)} %pad_maximum_fusion.5), channel_id=1, source_target_pairs={{0,32},{1,33},{2,34},{3,35},{4,36},{5,37},{6,38},{7,39},{8,40},{9,... | collective-permute-start | bytes 786440 | tf_op jit(solution)/shard_map/ppermute | solution.py:31
  986.6 116.4 %copy-start.15 = (f32[1,1,6,256,128]{3,4,2,1,0:T(8,128)S(1)}, f32[1,1,6,256,128]{3,4,2,1,0:T(8,128)}, u32[]{:S(2)}) copy-start(f32[1,1,6,256,128]{3,4,2,1,0:T(8,128)} %copy.409) | copy-start | bytes 2359300
  (8 other events, 10.6 us)
Sparse Core Ops, SparseCore 0:
  10.9 2.5 sort.21.cloned.1.call-done
  18.2 80.2 all-gather.3
  584.0 71.0 all-gather.5
  839.0 71.2 all-gather.7
  (1 shorter events, 0.0 us)
